TPU v7x, 256 devices: a whole 4x4x8 slice. The times are simulated.
256 devices in a mesh: dp: 16 (over z, core), filter: 16 (over x, y).
Axes of the slice: x: 4, y: 4, z: 8, core: 2. Of those that a mesh axis runs over, the one named last changes fastest.
Arguments:
- patches: bfloat16 [256, 48, 2048], P('filter', 'dp'), may hold values from -6 to 6
- cotangent: bfloat16 [256, 48, 2048], P('filter', 'dp'), may hold values from -6 to 6
- first_weight: bfloat16 [27, 256, 256], P(None, 'filter'), may hold values from -0.078125 to 0.078125
- second_weight: bfloat16 [27, 256, 256], P(None, 'filter'), may hold values from -0.078125 to 0.078125
- counts: int32 [16], P('dp'), may hold values from 0 to 3, as said below
Outputs:
- output_maps: float32 [256, 48, 2048], P('filter', 'dp')
- input_grad: float32 [256, 48, 2048], P('filter', 'dp')
- first_grad: float32 [27, 256, 256], P(None, 'filter')
- second_grad: float32 [27, 256, 256], P(None, 'filter')
Inputs may be any that keep to these rules, and one draw needn't show every extreme that they name: The counts of all groups sum to 16; one group holds exactly 3 live patches. Live patches of a group occupy its first slots.
All inputs are finite; a program needn't handle non-finite values.
Results may differ from a plain program's by a relative error of at most 0.0029.
Values may be sent and summed in bfloat16 or wider, within the bound.
No kernel may reach another device: no remote copies, remote signals or barrier semaphores. Data moves between devices by JAX's collectives and lax.ppermute only.
A program may use at most 128 MiB of HBM per device.

v0:
```python
import jax
import jax.numpy as jnp
from jax import lax
from jax.sharding import PartitionSpec as P

PX = 8
PY = 16
PZ = 16
CAP = 3
CELLS = 2048
stencil_taps = [(ox, oy, oz) for ox in (-1, 0, 1) for oy in (-1, 0, 1) for oz in (-1, 0, 1)]


def shift_cells(value, ox, oy, oz):
    span = PY * PZ + PZ + 1
    step = ox * PY * PZ + oy * PZ + oz
    padded = jnp.pad(value, [(0, 0)] * (value.ndim - 1) + [(span, span)])
    moved = lax.slice_in_dim(padded, span + step, span + step + CELLS, axis=value.ndim - 1)
    cell = jnp.arange(CELLS, dtype=jnp.int32)
    pos_x = cell // (PY * PZ) + ox
    pos_y = cell // PZ % PY + oy
    pos_z = cell % PZ + oz
    inside = (pos_x >= 0) & (pos_x < PX) & (pos_y >= 0) & (pos_y < PY) & (pos_z >= 0) & (pos_z < PZ)
    return jnp.where(inside, moved, jnp.zeros_like(moved))


def shifted_stack(value):
    return jnp.stack([shift_cells(value, -ox, -oy, -oz) for ox, oy, oz in stencil_taps])


def forward_conv(inputs, weight):
    proj = jnp.einsum("toi,isc->tosc", weight, inputs, preferred_element_type=jnp.float32)
    total = jnp.zeros(proj.shape[1:], jnp.float32)
    for t, (ox, oy, oz) in enumerate(stencil_taps):
        total = total + shift_cells(proj[t], ox, oy, oz)
    return total


def weight_conv(grads, inputs):
    stack = shifted_stack(grads)
    return jnp.einsum("tosc,isc->toi", stack, inputs, preferred_element_type=jnp.float32)


def backward_conv(grads, weight):
    stack = shifted_stack(grads)
    return lax.psum_scatter(
        jnp.einsum("toi,tosc->isc", weight, stack, preferred_element_type=jnp.float32),
        "filter",
        scatter_dimension=0,
        tiled=True,
    )


def layer_pair(inputs, masked, first_weight, second_weight):
    full_inputs = lax.all_gather(inputs, "filter", axis=0, tiled=True)
    first = forward_conv(full_inputs, first_weight)
    hidden = jax.nn.silu(first).astype(jnp.bfloat16)
    full_hidden = lax.all_gather(hidden, "filter", axis=0, tiled=True)
    result = forward_conv(full_hidden, second_weight)
    hidden_grad = backward_conv(masked, second_weight)
    second_part = weight_conv(masked, full_hidden)
    sigma = jax.nn.sigmoid(first)
    delta = (hidden_grad * sigma * (1.0 + first * (1.0 - sigma))).astype(jnp.bfloat16)
    in_grad = backward_conv(delta, first_weight)
    first_part = weight_conv(delta, full_inputs)
    return (result, in_grad, first_part, second_part)


def shards(patches, cotangent, first_weight, second_weight, counts):
    live = (jnp.arange(CAP, dtype=jnp.int32) < counts[0]).astype(jnp.bfloat16)
    masked = cotangent * live[None, :, None]
    result, in_grad, first_part, second_part = layer_pair(
        patches, masked, first_weight, second_weight
    )
    output_maps = result * live[None, :, None].astype(jnp.float32)
    first_sum, second_sum = lax.psum((first_part, second_part), "dp")
    scale = 1.0 / jnp.sqrt(jnp.float32(lax.axis_size("dp") * CELLS))
    return (output_maps, in_grad, first_sum * scale, second_sum * scale)


def solution(mesh):
    placed = (
        P("filter", "dp", None),
        P("filter", "dp", None),
        P(None, "filter", None),
        P(None, "filter", None),
        P("dp"),
    )
    return jax.shard_map(
        shards,
        mesh=mesh,
        in_specs=placed,
        out_specs=(
            P("filter", "dp", None),
            P("filter", "dp", None),
            P(None, "filter", None),
            P(None, "filter", None),
        ),
        check_vma=False,
    )
```

profile of v0, /device:TPU:1, one launch (start us, length us, event | category | flops | bytes accessed | tf_op | source)
XLA Modules:
  0.0 506.1 jit_solution(9480231245878165293)
XLA Ops:
  8.9 1.0 broadcast_multiply_fusion.2
  13.2 2.3 copy-done.2
  15.5 4.8 convolution_bitcast_fusion.2
  20.4 46.6 %all-gather.3.cloned.1.call-done = bf16[256,3,2048]{2,0,1:T(8,128)(2,1)} async-done(((bf16[16,3,2048]{2,0,1:T(8,128)(2,1)}), bf16[256,3,2048]{2,0,1:T(8,128)(2,1)}) %all-gather.3.cloned.1.call-update) | async-done | bytes 3145744 | tf_op jit(solution)/shard_map/all_gather | solution.py:55
  67.0 3.4 fusion.5
  70.7 3.9 copy-done.4
  74.5 3.0 slice_bitcast_fusion.53
  77.5 77.9 %reduce-scatter.2.cloned.1.call-done = f32[16,3,2048]{2,0,1:T(8,128)} async-done(((f32[256,3,2048]{2,0,1:T(8,128)}), f32[16,3,2048]{2,0,1:T(8,128)}) %reduce-scatter.2.cloned.1.call-update) | async-done | bytes 393232 | tf_op jit(solution)/shard_map/reduce_scatter | solution.py:46
  155.4 4.9 multiply_convert_fusion
  182.6 7.1 %convolution_bitcast_fusion.1 = f32[256,3,2048]{0,2,1:T(8,128)} fusion(bf16[27,16,3,2048]{3,1,2,0:T(8,128)(2,1)} %fusion.279, bf16[27,16,256]{2,1,0:T(8,128)(2,1)S(1)} %copy-done), kind=kOutput, calls=%fused_computation.1 | convolution fusion | flops 1358954496 | bytes 11821056 | tf_op jit(solution)/shard_map/toi,tosc->isc/dot_general | solution.py:47
  189.7 9.6 %copy.24 = f32[256,3,2048]{2,1,0:T(4,128)} copy(f32[256,3,2048]{0,2,1:T(8,128)} %convolution_bitcast_fusion.1) | data formatting | bytes 12582912 | tf_op jit(solution)/shard_map/toi,tosc->isc/dot_general | solution.py:47
  201.2 5.8 %fusion.7 = f32[27,16,256]{2,1,0:T(8,128)} fusion(bf16[27,16,3,2048]{3,1,2,0:T(8,128)(2,1)} %fusion.279, bf16[256,3,2048]{2,0,1:T(8,128)(2,1)} %all-gather.3.cloned.1.call-done), kind=kOutput, calls=%fused_computation.10 | convolution fusion | flops 1358954496 | bytes 8896512 | tf_op jit(solution)/shard_map/tosc,isc->toi/dot_general | solution.py:41
  207.0 21.6 %all-gather.5.cloned.1.call-done = bf16[256,3,2048]{2,0,1:T(8,128)(2,1)} async-done(((bf16[16,3,2048]{2,0,1:T(8,128)(2,1)}), bf16[256,3,2048]{2,0,1:T(8,128)(2,1)}) %all-gather.5.cloned.1.call-update) | async-done | bytes 3145744 | tf_op jit(solution)/shard_map/all_gather | solution.py:58
  228.6 3.5 convolution_bitcast_fusion
  232.1 4.1 copy-done.3
  236.4 1.7 copy-done.7
  238.1 4.8 fusion.10
  242.9 6.1 %slice_bitcast_fusion.26 = (f32[16,3,2048]{2,0,1:T(8,128)S(1)}, f32[16,3,2048]{2,0,1:T(8,128)}, f32[16,3,2048]{2,0,1:T(8,128)}, f32[16,3,2048]{2,0,1:T(8,128)}, ...) fusion(f32[27,16,3,2048]{3,1,2,0:T(8,128)} %copy-done.3), kind=kLoop, calls=%fused_computation.196 | loop fusion | bytes 14942208 | tf_op jit(solution)/shard_map/squeeze | solution.py:35
  249.0 6.4 %fusion.115 = f32[16,3,2048]{2,0,1:T(8,128)} fusion(f32[16,3,2048]{2,0,1:T(8,128)} %get-tuple-element.19, f32[16,3,2048]{2,0,1:T(8,128)} %get-tuple-element.18, f32[16,3,2048]{2,0,1:T(8,128)} %get-tuple-element.17, f32[16,3,2048]{2,0,1:T(8,128)} %get-tuple-element.20, f32[16,3,2048]{2,0,1:T(8,128)} %get-tuple-element.21, ...), kind=kLoop, calls=%fused_computation.166 | loop fusion | flops 5308416 | bytes 11065356 | tf_op jit(solution)/shard_map/mul | solution.py:75
  255.4 127.1 %all-reduce.59.cloned.1.call-done = f32[256,3,2048]{2,1,0:T(4,128)} async-done(((f32[256,3,2048]{2,1,0:T(4,128)}), f32[256,3,2048]{2,1,0:T(4,128)}) %all-reduce.59.cloned.1.call-update) | async-done | bytes 6291472
  382.5 1.1 constant_dynamic-slice_fusion
  384.6 111.3 %all-reduce.61.cloned.1.call-done = (f32[27,16,256]{2,1,0:T(8,128)}, f32[27,16,256]{2,1,0:T(8,128)}) async-done(((f32[27,16,256]{2,1,0:T(8,128)}, f32[27,16,256]{2,1,0:T(8,128)}), (f32[27,16,256]{2,1,0:T(8,128)}, f32[27,16,256]{2,1,0:T(8,128)})) %all-reduce.61.cloned.1.call-update) | async-done | bytes 884752 | tf_op jit(solution)/shard_map/psum | solution.py:76
  495.9 1.8 broadcast_multiply_fusion
  497.7 1.8 broadcast_multiply_fusion.1
  (99 shorter events, 28.9 us)
Async XLA Ops:
  7.2 59.8 %copy-start = (bf16[27,16,256]{2,1,0:T(8,128)(2,1)S(1)}, bf16[27,16,256]{2,1,0:T(8,128)(2,1)}, u32[]{:S(2)}) copy-start(bf16[27,16,256]{2,1,0:T(8,128)(2,1)} %param.7) | copy-start | bytes 663556
  7.2 4.3 copy-start.5
  7.2 59.8 %all-gather.3.cloned.1.call-start = ((), (), s32[]{:S(2)}) async-start(), calls=%async_computation.1 | async-start | bytes 3342336 | tf_op jit(solution)/shard_map/all_gather | solution.py:55
  7.9 147.5 %reduce-scatter.2.cloned.1.call-start = ((), (), s32[]{:S(2)}) async-start(), calls=%async_computation.3 | async-start | bytes 6684672 | tf_op jit(solution)/shard_map/reduce_scatter | solution.py:46
  9.9 5.6 %copy-start.6 = (bf16[27,16,256]{2,1,0:T(8,128)(2,1)S(1)}, bf16[27,16,256]{2,1,0:T(8,128)(2,1)}, u32[]{:S(2)}) copy-start(bf16[27,16,256]{2,1,0:T(8,128)(2,1)} %param.8) | copy-start | bytes 663556
  13.2 2.3 copy-start.2
  20.3 208.3 %all-gather.5.cloned.1.call-start = ((), (), s32[]{:S(2)}) async-start(), calls=%async_computation.2 | async-start | bytes 3342336 | tf_op jit(solution)/shard_map/all_gather | solution.py:58
  70.5 4.1 copy-start.4
  175.3 207.2 %all-reduce.59.cloned.1.call-start = ((), (), s32[]{:S(2)}) async-start(), calls=%async_computation.4 | async-start | bytes 16777216
  199.3 0.7 copy-start.8
  199.3 296.6 %all-reduce.61.cloned.1.call-start = ((), (), s32[]{:S(2)}) async-start(), calls=%async_computation.5 | async-start | bytes 1769472 | tf_op jit(solution)/shard_map/psum | solution.py:76
  232.1 4.1 copy-start.3
  236.2 1.9 copy-start.7
  249.0 250.6 %copy-start.1 = (bf16[27,16,256]{2,1,0:T(8,128)(2,1)S(1)}, bf16[27,16,256]{2,1,0:T(8,128)(2,1)}, u32[]{:S(2)}) copy-start(bf16[27,16,256]{2,1,0:T(8,128)(2,1)} %param.7) | copy-start | bytes 663556
Sparse Core Ops, SparseCore 0:
  10.5 56.4 all-gather.2
  70.7 84.6 reduce-scatter.1
  175.4 53.1 all-gather.4
  232.0 150.3 all-reduce.58
  385.5 110.4 all-reduce.60
where the time goes:
time: 507 us; the launch traced here: 506 us
  waiting for transfers between devices  385 us (76%)
  other arithmetic  41.3 us (8%)
  local copies, waits for them, and re-layouts  34.3 us (7%)
  matrix products  29.5 us (6%)
  between operations  15.5 us (3%)
    unnamed x6, waiting for transfers between devices  128 us
    psum x1, waiting for transfers between devices, shards(): first_sum, second_sum = lax.psum((first_part, second_part), 'dp')  111 us
    reduce_scatter x1, waiting for transfers between devices, backward_conv(): lax.psum_scatter(jnp.einsum('toi,tosc->isc', weight, stack, preferred_ele...  77.9 us
    all_gather x1, waiting for transfers between devices, layer_pair(): full_inputs = lax.all_gather(inputs, 'filter', axis=0, tiled=True)  46.6 us
    unnamed x52, other arithmetic  23.4 us
    all_gather x1, waiting for transfers between devices, layer_pair(): full_hidden = lax.all_gather(hidden, 'filter', axis=0, tiled=True)  21.6 us
    unnamed x21, local copies, waits for them, and re-layouts  15.2 us
    dot_general x2, matrix products, backward_conv(): jnp.einsum('toi,tosc->isc', weight, stack, preferred_element_type=jnp.flo...  11.9 us
  transfers between devices with their start and end apart: 5, of which 5 were waited for; matrix products, arithmetic and copies ran while one was open for 14% of the time, Pallas kernels for 0%

commit v1 on v0

--- a/solution.py
+++ b/solution.py
@@ -55,7 +55,10 @@
     full_inputs = lax.all_gather(inputs, "filter", axis=0, tiled=True)
     first = forward_conv(full_inputs, first_weight)
     hidden = jax.nn.silu(first).astype(jnp.bfloat16)
-    full_hidden = lax.all_gather(hidden, "filter", axis=0, tiled=True)
+    group_loops_on = lambda z_in: jnp.concatenate(
+        lax.all_to_all(jnp.stack(lax.axis_size("filter") * [z_in]), "filter", 0, 0), axis=0
+    )
+    full_hidden = group_loops_on(hidden)
     result = forward_conv(full_hidden, second_weight)
     hidden_grad = backward_conv(masked, second_weight)
     second_part = weight_conv(masked, full_hidden)

time: 507 us -> 497 us (0.980)
  other arithmetic: 41.3 us -> 23.3 us
  waiting for transfers between devices: 385 us -> 393 us
    all_to_all x0 -> x1, waiting for transfers between devices: none -> 26.1 us  [layer_pair(): lax.all_to_all(jnp.stack(lax.axis_size('filter') * [z_in]), 'filter', 0, 0)]
    unnamed x6 -> x5, waiting for transfers between devices: 128 us -> 153 us
    all_gather x1 -> x0, waiting for transfers between devices: 21.6 us -> none  [layer_pair(): full_hidden = lax.all_gather(hidden, 'filter', axis=0, tiled=True)]
    psum x1, waiting for transfers between devices: 111 us -> 90.1 us  [shards(): first_sum, second_sum = lax.psum((first_part, second_part), 'dp')]
    unnamed x52, other arithmetic: 23.4 us -> 9.26 us
    unnamed x21 -> x17, local copies, waits for them, and re-layouts: 15.2 us -> 11.9 us
  transfers between devices with their start and end apart: 5 -> 5, of which waited for: 5 -> 5; matrix products, arithmetic and copies ran while one was open for 14% -> 11% of each run, Pallas kernels for 0% -> 0%
where the time goes in v1:
time: 497 us; the launch traced here: 496 us
  waiting for transfers between devices  393 us (79%)
  local copies, waits for them, and re-layouts  30.1 us (6%)
  matrix products  28.6 us (6%)
  other arithmetic  23.3 us (5%)
  between operations  15.6 us (3%)
  starting transfers between devices  4.98 us (1%)
    unnamed x5, waiting for transfers between devices  153 us
    psum x1, waiting for transfers between devices, shards(): first_sum, second_sum = lax.psum((first_part, second_part), 'dp')  90.1 us
    reduce_scatter x1, waiting for transfers between devices, backward_conv(): lax.psum_scatter(jnp.einsum('toi,tosc->isc', weight, stack, preferred_ele...  77.9 us
    all_gather x1, waiting for transfers between devices, layer_pair(): full_inputs = lax.all_gather(inputs, 'filter', axis=0, tiled=True)  46.6 us
    all_to_all x1, waiting for transfers between devices, layer_pair(): lax.all_to_all(jnp.stack(lax.axis_size('filter') * [z_in]), 'filter', 0, 0)  26.1 us
    dot_general x2, matrix products, backward_conv(): jnp.einsum('toi,tosc->isc', weight, stack, preferred_element_type=jnp.flo...  11.9 us
    unnamed x17, local copies, waits for them, and re-layouts  11.9 us
    dot_general x2, matrix products, weight_conv(): jnp.einsum('tosc,isc->toi', stack, inputs, preferred_element_type=jnp.flo...  10.7 us
  transfers between devices with their start and end apart: 5, of which 5 were waited for; matrix products, arithmetic and copies ran while one was open for 11% of the time, Pallas kernels for 0%

profile of v1, /device:TPU:1, one launch (start us, length us, event | category | flops | bytes accessed | tf_op | source)
XLA Modules:
  0.0 495.8 jit_solution(17488840797564924927)
XLA Ops:
  13.2 2.3 copy-done.1
  15.5 4.8 convolution_bitcast_fusion.2
  20.4 46.6 %all-gather.2.cloned.1.call-done = bf16[256,3,2048]{2,0,1:T(8,128)(2,1)} async-done(((bf16[16,3,2048]{2,0,1:T(8,128)(2,1)}), bf16[256,3,2048]{2,0,1:T(8,128)(2,1)}) %all-gather.2.cloned.1.call-update) | async-done | bytes 3145744 | tf_op jit(solution)/shard_map/all_gather | solution.py:55
  67.0 3.4 fusion.2
  70.7 3.9 copy-done.2
  74.5 3.0 slice_bitcast_fusion.53
  77.5 77.9 %reduce-scatter.2.cloned.1.call-done = f32[16,3,2048]{2,0,1:T(8,128)} async-done(((f32[256,3,2048]{2,0,1:T(8,128)}), f32[16,3,2048]{2,0,1:T(8,128)}) %reduce-scatter.2.cloned.1.call-update) | async-done | bytes 393232 | tf_op jit(solution)/shard_map/reduce_scatter | solution.py:46
  155.4 4.9 multiply_convert_fusion
  162.9 2.3 copy-done.5
  165.3 2.0 stack.114
  167.3 4.6 all-to-all-start
  177.0 5.8 %fusion.4 = f32[27,16,256]{2,1,0:T(8,128)} fusion(bf16[27,16,3,2048]{3,1,2,0:T(8,128)(2,1)} %fusion.273, bf16[256,3,2048]{2,0,1:T(8,128)(2,1)} %all-gather.2.cloned.1.call-done), kind=kOutput, calls=%fused_computation.7 | convolution fusion | flops 1358954496 | bytes 8896512 | tf_op jit(solution)/shard_map/tosc,isc->toi/dot_general | solution.py:41
  182.8 26.1 %all-to-all-done = bf16[16,16,3,2048]{3,1,2,0:T(8,128)(2,1)} async-done(((bf16[16,16,3,2048]{3,1,2,0:T(8,128)(2,1)}), bf16[16,16,3,2048]{3,1,2,0:T(8,128)(2,1)}, u32[]{:S(2)}, u32[]{:S(2)}) %all-to-all-start) | async-done | bytes 3145760 | tf_op jit(solution)/shard_map/all_to_all | solution.py:59
  208.9 2.1 copy.17
  211.0 4.8 convolution_bitcast_fusion.3
  215.9 7.1 %convolution_bitcast_fusion.1 = f32[256,3,2048]{0,2,1:T(8,128)} fusion(bf16[27,16,3,2048]{3,1,2,0:T(8,128)(2,1)} %fusion.273, bf16[27,16,256]{2,1,0:T(8,128)(2,1)S(1)} %copy-done), kind=kOutput, calls=%fused_computation.1 | convolution fusion | flops 1358954496 | bytes 11821056 | tf_op jit(solution)/shard_map/toi,tosc->isc/dot_general | solution.py:47
  223.0 9.7 %copy.25 = f32[256,3,2048]{2,1,0:T(4,128)} copy(f32[256,3,2048]{0,2,1:T(8,128)} %convolution_bitcast_fusion.1) | data formatting | bytes 12582912 | tf_op jit(solution)/shard_map/toi,tosc->isc/dot_general | solution.py:47
  234.6 2.6 convolution_bitcast_fusion
  238.4 3.2 fusion.109
  241.7 90.1 %all-reduce.61.cloned.1.call-done = (f32[27,16,256]{2,1,0:T(8,128)}, f32[27,16,256]{2,1,0:T(8,128)}) async-done(((f32[27,16,256]{2,1,0:T(8,128)}, f32[27,16,256]{2,1,0:T(8,128)}), (f32[27,16,256]{2,1,0:T(8,128)}, f32[27,16,256]{2,1,0:T(8,128)})) %all-reduce.61.cloned.1.call-update) | async-done | bytes 884752 | tf_op jit(solution)/shard_map/psum | solution.py:79
  331.7 1.8 broadcast_multiply_fusion
  333.6 1.8 broadcast_multiply_fusion.1
  335.4 151.8 %all-reduce.59.cloned.1.call-done = f32[256,3,2048]{2,1,0:T(4,128)} async-done(((f32[256,3,2048]{2,1,0:T(4,128)}), f32[256,3,2048]{2,1,0:T(4,128)}) %all-reduce.59.cloned.1.call-update) | async-done | bytes 6291472
  487.2 1.1 constant_dynamic-slice_fusion
  (96 shorter events, 16.2 us)
Async XLA Ops:
  7.2 59.8 %copy-start = (bf16[27,16,256]{2,1,0:T(8,128)(2,1)S(1)}, bf16[27,16,256]{2,1,0:T(8,128)(2,1)}, u32[]{:S(2)}) copy-start(bf16[27,16,256]{2,1,0:T(8,128)(2,1)} %param.7) | copy-start | bytes 663556
  7.2 4.3 copy-start.3
  7.2 59.8 %all-gather.2.cloned.1.call-start = ((), (), s32[]{:S(2)}) async-start(), calls=%async_computation.2 | async-start | bytes 3342336 | tf_op jit(solution)/shard_map/all_gather | solution.py:55
  7.9 147.5 %reduce-scatter.2.cloned.1.call-start = ((), (), s32[]{:S(2)}) async-start(), calls=%async_computation.3 | async-start | bytes 6684672 | tf_op jit(solution)/shard_map/reduce_scatter | solution.py:46
  9.9 5.6 %copy-start.4 = (bf16[27,16,256]{2,1,0:T(8,128)(2,1)S(1)}, bf16[27,16,256]{2,1,0:T(8,128)(2,1)}, u32[]{:S(2)}) copy-start(bf16[27,16,256]{2,1,0:T(8,128)(2,1)} %param.8) | copy-start | bytes 663556
  13.2 2.3 copy-start.1
  70.5 4.1 copy-start.2
  162.8 2.4 copy-start.5
  167.3 41.5 %all-to-all-start = ((bf16[16,16,3,2048]{3,1,2,0:T(8,128)(2,1)}), bf16[16,16,3,2048]{3,1,2,0:T(8,128)(2,1)}, u32[]{:S(2)}, u32[]{:S(2)}) async-start(bf16[16,16,3,2048]{3,1,2,0:T(8,128)(2,1)} %stack.114), calls=%async_computation | async-start | bytes 6291456 | tf_op jit(solution)/shard_map/all_to_all | solution.py:59
  172.0 159.7 %all-reduce.61.cloned.1.call-start = ((), (), s32[]{:S(2)}) async-start(), calls=%async_computation.5 | async-start | bytes 1769472 | tf_op jit(solution)/shard_map/psum | solution.py:79
  215.9 271.3 %all-reduce.59.cloned.1.call-start = ((), (), s32[]{:S(2)}) async-start(), calls=%async_computation.4 | async-start | bytes 16777216
  232.7 0.7 copy-start.6
Sparse Core Ops, SparseCore 0:
  10.5 56.4 all-gather.1
  70.7 84.6 reduce-scatter.1
  216.0 115.7 all-reduce.60
  335.6 151.5 all-reduce.58
